TPU v7x, 128 devices: a whole 4x4x4 slice. The times are simulated.
128 devices in a mesh: lat: 8 (over z, core), lon: 16 (over x, y).
Axes of the slice: x: 4, y: 4, z: 4, core: 2. Of those that a mesh axis runs over, the one named last changes fastest.
Arguments:
- tracers: float32 [2, 48, 1024, 2048], P(None, None, 'lat', 'lon'), may hold values from -6 to 6
- east_courant: float32 [48, 1024, 2048], P(None, 'lat', 'lon'), may hold values from -0.4 to 0.4
- north_courant: float32 [48, 1024, 2048], P(None, 'lat', 'lon'), may hold values from -0.4 to 0.4
- diffusivity: float32 [48, 1024, 2048], P(None, 'lat', 'lon'), may hold values from 0.05 to 20
- land_sea: int32 [1024, 2048], P('lat', 'lon'), may hold values 0 or 1
- fluxes: float32 [6, 1048576], P(None, ('lat', 'lon')), may hold values from -6 to 6
- source_cell: int32 [128, 4, 6144], P(('lat', 'lon')), may hold values from 0 to 8191, as said below
- link_weight: float32 [128, 4, 6144], P(('lat', 'lon')), may hold values from 0.05 to 0.3
- target_cell: int32 [128, 4, 6144], P(('lat', 'lon')), may hold values from 0 to 16383, as said below
Outputs:
- stepped: float32 [2, 48, 1024, 2048], P(None, None, 'lat', 'lon')
Inputs may be any that keep to these rules, and one draw needn't show every extreme that they name: source_cell[s, n, c] lies in n * 2048 to (n+1) * 2048 - 1; several links may name the same cells. target_cell[d, n, c] has its row in (1 - n // 2) * 64 to that plus 128 // 2 - 1 and its column in (1 - n % 2) * 64 to that plus 128 // 2 - 1.
All inputs are finite; a program needn't handle non-finite values. No bound on the sum of `land_sea` on one device may be relied on, other than what follows from the above.
Results may differ from a plain program's by a relative error of at most 0.00005.
Values sent between devices are 32-bit elements; how exact they have to be, the bound alone decides.
A program may use at most 192 MiB of HBM per device.

v0:
```python
import math
import jax, jax.numpy as jnp
import numpy as np
from jax import lax
from jax.experimental import pallas as pl
from jax.experimental.pallas import tpu as pltpu
from jax.sharding import PartitionSpec as P

LEVELS = 48
HALF = 24
R = 32
G = 8
PAD = 8


def stencil_weights():
    cols = 128
    main = np.zeros((cols, 2 * cols), np.float32)
    for i in range(cols):
        for off, w in ((-1, -1), (0, 7), (1, 7), (2, -1)):
            if 0 <= i + off < cols:
                main[i + off, i] = w
        for off, w in ((-2, -1), (-1, 7), (0, 7), (1, -1)):
            if 0 <= i + off < cols:
                main[i + off, cols + i] = w
    halves = []
    for half in range(2):
        edge = np.zeros((cols, 2 * cols), np.float32)
        order = (-2, -1, 128, 129) if half == 0 else (128, 129, -2, -1)
        for lane in range(cols):
            p = order[lane % 4]
            for i in range(cols):
                edge[lane, i] = {-1: -1, 0: 7, 1: 7, 2: -1}.get(p - i, 0)
                edge[lane, cols + i] = {-2: -1, -1: 7, 0: 7, 1: -1}.get(p - i, 0)
        halves.append(np.concatenate([main, main, edge, edge], 0))
    return jnp.asarray(np.stack(halves), jnp.bfloat16)


def two_pieces(x):
    high = x.astype(jnp.bfloat16)
    return high, (x - high.astype(jnp.float32)).astype(jnp.bfloat16)


def column_kernel(tr_hbm, ec_hbm, nc_hbm, df_hbm, w_ref, land_ref, surf_ref, pe_ref, pw_ref, south_ref, north_ref, ncs_ref,
                  out_hbm, T, EC, NC, DF, C, OUT, H, X, S, FN, in_sem, out_sem):
    rows, cols = 128, 128
    blocks = rows // R

    def loads(b):
        r = pl.multiple_of(b * R, R)
        return [
            pltpu.make_async_copy(tr_hbm.at[:, :, pl.ds(r, R), :], T.at[:, :, pl.ds(r + PAD, R), :], in_sem.at[b, 0]),
            pltpu.make_async_copy(ec_hbm.at[:, pl.ds(r, R), :], EC.at[:, pl.ds(r, R), :], in_sem.at[b, 1]),
            pltpu.make_async_copy(nc_hbm.at[:, pl.ds(r, R), :], NC.at[:, pl.ds(r, R), :], in_sem.at[b, 2]),
            pltpu.make_async_copy(df_hbm.at[:, pl.ds(r, R), :], DF.at[:, pl.ds(r, R), :], in_sem.at[b, 3]),
        ]

    def start(b, carry):
        for c in loads(b):
            c.start()
        return carry

    lax.fori_loop(0, blocks, start, 0)

    lane = lax.broadcasted_iota(jnp.int32, (rows, cols), 1)
    low = lane % 4 < 2
    for t in range(2):
        pe, pw = pe_ref[t], pw_ref[t]
        for half in range(2):
            h = jnp.where(low, pw, pe) if half == 0 else jnp.where(low, pe, pw)
            H[t, half, 0], H[t, half, 1] = two_pieces(h)

    for c in loads(0):
        c.wait()

    def edges(k, carry):
        for t in range(2):
            T[t, k, PAD - 2:PAD, :] = south_ref[t, k]
            T[t, k, PAD + rows:PAD + rows + 2, :] = north_ref[t, k]
            s = T[t, k, PAD - 2:PAD - 1, :] + T[t, k, PAD + 1:PAD + 2, :]
            m = T[t, k, PAD - 1:PAD, :] + T[t, k, PAD:PAD + 1, :]
            FN[t, k, PAD - 1:PAD, :] = ncs_ref[k] * (7.0 * m - s)
        return carry

    lax.fori_loop(0, LEVELS, edges, 0)

    def block(b, carry):
        @pl.when(b + 1 < blocks)
        def _():
            for c in loads(b + 1):
                c.wait()

        r = pl.multiple_of(b * R, R)
        rr = pl.ds(r, R)
        lane = lax.broadcasted_iota(jnp.int32, (R, cols), 1)
        first = lane == 0
        stress = 2.0 * jnp.sqrt(surf_ref[3, rr, :] * surf_ref[3, rr, :] + surf_ref[4, rr, :] * surf_ref[4, rr, :])

        for half in range(2):
            def group(q, carry):
                for u in range(G):
                    j = q * G + u
                    k = half * HALF + j
                    here = (lane + 2 * half) % cols // 4 == j
                    for t in range(2):
                        x = T[t, k, pl.ds(r + PAD, R), :]
                        at = pl.ds((u * 2 + t) * R, R)
                        X[at, 0:cols], X[at, cols:2 * cols] = two_pieces(x)
                        for p in range(2):
                            h = H[t, half, p, rr, :]
                            X[at, (2 + p) * cols:(3 + p) * cols] = jnp.where(here, h, jnp.zeros_like(h))
                S[...] = jnp.dot(X[...], w_ref[half], preferred_element_type=jnp.float32)
                for u in range(G):
                    j = q * G + u
                    k = half * HALF + j
                    ce = EC[k, rr, :]
                    cn = NC[k, rr, :]
                    hec = pltpu.roll(pw_ref[half, rr, :], cols - 96 - j, 1)
                    cw = jnp.where(first, hec, pltpu.roll(ce, 1, 1))
                    for t in range(2):
                        at = pl.ds((u * 2 + t) * R, R)
                        x = T[t, k, pl.ds(r + PAD, R), :]
                        n1 = T[t, k, pl.ds(r + PAD + 1, R), :]
                        n2 = T[t, k, pl.ds(r + PAD + 2, R), :]
                        s1 = T[t, k, pl.ds(r + PAD - 1, R), :]
                        fn = cn * (7.0 * (x + n1) - (s1 + n2))
                        FN[t, k, pl.ds(r + PAD, R), :] = fn
                        fs = FN[t, k, pl.ds(r + PAD - 1, R), :]
                        div = (ce * S[at, 0:cols] - cw * S[at, cols:2 * cols]) + (fn - fs)
                        OUT[t, k, rr, :] = x - div * (1.0 / 12.0)
                return carry

            lax.fori_loop(0, HALF // G, group, 0)

        heat = 0.5 * surf_ref[2, rr, :]
        tops = [0.5 * surf_ref[0, rr, :], 0.5 * surf_ref[1, rr, :]]
        above = None
        cprev = None
        vprev = [None, None]
        for k in range(LEVELS):
            if k < LEVELS - 1:
                below = DF[k, rr, :] + stress * math.exp(-4.0 * k / LEVELS)
            absorb = math.exp(-4.0 * k / LEVELS) - math.exp(-4.0 * (k + 1) / LEVELS)
            adv = [OUT[0, k, rr, :] + heat * absorb, OUT[1, k, rr, :]]
            if k == 0:
                adv[0] = adv[0] + tops[0]
                adv[1] = adv[1] + tops[1]
                inv = 1.0 / (1.0 + below)
                v = [adv[0] * inv, adv[1] * inv]
            else:
                pivot = 1.0 + above * (1.0 - cprev)
                if k < LEVELS - 1:
                    pivot = pivot + below
                inv = 1.0 / pivot
                v = [(adv[t] + above * vprev[t]) * inv for t in range(2)]
            if k < LEVELS - 1:
                cprev = below * inv
                C[k] = cprev
                above = below
                for t in range(2):
                    OUT[t, k, rr, :] = v[t]
            vprev = v
        sea = land_ref[rr, :] == 1
        x = vprev
        for k in range(LEVELS - 1, -1, -1):
            if k < LEVELS - 1:
                c = C[k]
                x = [OUT[t, k, rr, :] + c * x[t] for t in range(2)]
            for t in range(2):
                OUT[t, k, rr, :] = jnp.where(sea, x[t], T[t, k, pl.ds(r + PAD, R), :])
        pltpu.make_async_copy(OUT.at[:, :, rr, :], out_hbm.at[:, :, rr, :], out_sem.at[b]).start()
        return carry

    lax.fori_loop(0, blocks, block, 0)

    def drain(b, carry):
        rr = pl.ds(pl.multiple_of(b * R, R), R)
        pltpu.make_async_copy(OUT.at[:, :, rr, :], out_hbm.at[:, :, rr, :], out_sem.at[b]).wait()
        return carry

    lax.fori_loop(0, blocks, drain, 0)


def column_step(tracers, ec, nc, df, land, surf, pe, pw, south, north, ncs):
    any_ = pl.BlockSpec(memory_space=pl.ANY)
    vm = pl.BlockSpec(memory_space=pltpu.VMEM)
    blocks = 128 // R
    f = jnp.float32
    return pl.pallas_call(
        column_kernel,
        out_shape=jax.ShapeDtypeStruct(tracers.shape, f),
        in_specs=[any_] * 4 + [vm] * 8,
        out_specs=any_,
        scratch_shapes=[
            pltpu.VMEM((2, LEVELS, 144, 128), f),
            pltpu.VMEM((LEVELS, 128, 128), f),
            pltpu.VMEM((LEVELS, 128, 128), f),
            pltpu.VMEM((LEVELS, 128, 128), f),
            pltpu.VMEM((LEVELS, R, 128), f),
            pltpu.VMEM((2, LEVELS, 128, 128), f),
            pltpu.VMEM((2, 2, 2, 128, 128), jnp.bfloat16),
            pltpu.VMEM((2 * G * R, 512), jnp.bfloat16),
            pltpu.VMEM((2 * G * R, 256), f),
            pltpu.VMEM((2, LEVELS, 136, 128), f),
            pltpu.SemaphoreType.DMA((blocks, 4)),
            pltpu.SemaphoreType.DMA((blocks,)),
        ],
        compiler_params=pltpu.CompilerParams(vmem_limit_bytes=52 << 20),
        name="column_step",
    )(tracers, ec, nc, df, stencil_weights(), land, surf, pe, pw, south, north, ncs)
FIELDS = 5
CAP_ROWS = 48
SRC0 = 80
WGT0 = 128
LINK_ROWS = 176
MESH = pl.DeviceIdType.MESH


def exchange_kernel(tr_hbm, ec_hbm, nc_hbm, flux_ref, src_ref, wgt_ref, tgt_ref,
                    surf_ref, pe_ref, pw_ref, south_ref, north_ref, ncs_ref,
                    T, EC, NC, L, RL, TG, WP, Z, B, Q, pe_out, pw_out, rows_out, nc_out, load_sem, send_sem, recv_sem):
    rows, cols = 128, 128
    lat, lon = lax.axis_index("lat"), lax.axis_index("lon")
    nlat, nlon = lax.axis_size("lat"), lax.axis_size("lon")
    north, south = lax.rem(lat + 1, nlat), lax.rem(lat + nlat - 1, nlat)
    east, west = lax.rem(lon + 1, nlon), lax.rem(lon + nlon - 1, nlon)

    loads = [
        pltpu.make_async_copy(tr_hbm, T, load_sem.at[0]),
        pltpu.make_async_copy(ec_hbm, EC, load_sem.at[1]),
        pltpu.make_async_copy(nc_hbm.at[:, rows - 8:rows, :], NC, load_sem.at[2]),
    ]
    for c in loads:
        c.start()

    barrier = pltpu.get_barrier_semaphore()
    for peer in ((lat, east), (lat, west), (north, lon), (south, lon), (north, east), (south, west)):
        pl.semaphore_signal(barrier, inc=1, device_id=peer, device_id_type=MESH)

    field = lax.broadcasted_iota(jnp.int32, (8, cols), 0)
    for n in range(4):
        for h in range(16):
            lanes = pl.ds(n * 2048 + h * 128, 128)
            tile = flux_ref[0:6, lanes]
            more = jnp.where(field[0:5] == 1, jnp.broadcast_to(tile[5:6], (5, cols)), 0.0)
            L[n, h * FIELDS:(h + 1) * FIELDS, :] = tile[0:5] + more
        for j in range(CAP_ROWS):
            lanes = pl.ds(j * 128, 128)
            L[n, SRC0 + j:SRC0 + j + 1, :] = (src_ref[0, n:n + 1, lanes] - n * 2048).astype(jnp.float32)
            L[n, WGT0 + j:WGT0 + j + 1, :] = wgt_ref[0, n:n + 1, lanes]
            TG[n, j:j + 1, :] = tgt_ref[0, n:n + 1, lanes]

    pl.semaphore_wait(barrier, 6)

    def send(src, dst, at, peer):
        copy = pltpu.make_async_remote_copy(
            src_ref=src, dst_ref=dst, send_sem=send_sem.at[at], recv_sem=recv_sem.at[at],
            device_id=peer, device_id_type=MESH)
        copy.start()
        return copy

    links = {
        1: send(L.at[1], RL.at[0], 0, (lat, east)),
        2: send(L.at[2], RL.at[1], 1, (north, lon)),
        3: send(L.at[3], RL.at[2], 2, (north, east)),
    }

    sub16 = lax.broadcasted_iota(jnp.int32, (16, cols), 0).astype(jnp.float32)

    def remap(n, box):
        exists = jnp.where(lat >= n // 2, 1.0, 0.0)

        def pick(g, carry):
            at = pl.ds(pl.multiple_of(g * 8, 8), 8)
            cell = box[pl.ds(pl.multiple_of(SRC0 + g * 8, 8), 8), :].astype(jnp.int32)
            weight = box[pl.ds(pl.multiple_of(WGT0 + g * 8, 8), 8), :] * exists
            low = cell & 127
            high = cell >> 7
            for f in range(FIELDS):
                got = jnp.zeros((8, cols), jnp.float32)
                for h in range(16):
                    row = jnp.broadcast_to(box[h * FIELDS + f:h * FIELDS + f + 1, :], (8, cols))
                    got = jnp.where(high == h, jnp.take_along_axis(row, low, axis=1), got)
                got = got * weight
                top = got.astype(jnp.bfloat16).astype(jnp.float32)
                WP[f, at, :] = top
                WP[FIELDS + f, at, :] = got - top
            return carry

        lax.fori_loop(0, CAP_ROWS // 8, pick, 0)

        def hot(q, carry):
            for u in range(4):
                j = q * 4 + u
                lanes = pl.ds(pl.multiple_of(j * 128, 128), 128)
                cell = TG[n, pl.ds(j, 1), :]
                row = (cell >> 7) & 63
                col = cell & 63
                a = jnp.broadcast_to((row >> 2).astype(jnp.float32), (16, cols)) == sub16
                b = jnp.broadcast_to((((row & 3) << 6) + col).astype(jnp.float32), (16, cols))
                for w in range(2 * FIELDS):
                    v = jnp.broadcast_to(WP[w, pl.ds(j, 1), :], (16, cols))
                    Z[w * 16:(w + 1) * 16, lanes] = jnp.where(a, v, 0.0).astype(jnp.bfloat16)
                for s in range(16):
                    B[s * 16:(s + 1) * 16, lanes] = jnp.where(b == sub16 + 16.0 * s, 1.0, 0.0).astype(jnp.bfloat16)
            return carry

        lax.fori_loop(0, CAP_ROWS // 4, hot, 0)
        quad = lax.dot_general(Z[...], B[...], (((1,), (1,)), ((), ())), preferred_element_type=jnp.float32)
        col0 = (1 - n % 2) * 64
        for f in range(FIELDS):
            total = quad[f * 16:(f + 1) * 16] + quad[(FIELDS + f) * 16:(FIELDS + f + 1) * 16]
            for i in range(4):
                part = total[:, (i // 2) * 128:(i // 2 + 1) * 128]
                if (i % 2) * 64 != col0:
                    part = pltpu.roll(part, 64, 1)
                Q[n, f, i] = part

    remap(0, L.at[0])

    for c in loads:
        c.wait()
    lane = lax.broadcasted_iota(jnp.int32, (64, cols), 1)
    for t in range(2):
        for z in range(2):
            rr = pl.ds(z * 64, 64)

            def pack(q, carry):
                pe, pw = carry
                for u in range(8):
                    k = q * 8 + u
                    half = k // HALF
                    j = k - half * HALF
                    by = 4 * j + 2 * (1 - half)
                    y = pltpu.roll(T[t, k, rr, :], by, 1)
                    off = (lane - by) & 127
                    pe = jnp.where(off < 2, y, pe)
                    pw = jnp.where(off >= 126, y, pw)
                return pe, pw

            zero = jnp.zeros((64, cols), jnp.float32)
            pe, pw = lax.fori_loop(0, LEVELS // 8, pack, (zero, zero))

            def pack_courant(q, pw):
                for u in range(8):
                    j = q * 8 + u
                    y = pltpu.roll(EC[t * HALF + j, rr, :], j + 97, 1)
                    pw = jnp.where(lane == 96 + j, y, pw)
                return pw

            pw = lax.fori_loop(0, HALF // 8, pack_courant, pw)
            pe_out[t, rr, :] = pe
            pw_out[t, rr, :] = pw

    def edge_rows(k, carry):
        for t in range(2):
            rows_out[0, t, k] = T[t, k, 0:2, :]
            rows_out[1, t, k] = T[t, k, rows - 2:rows, :]
        nc_out[k] = NC[k, 7:8, :]
        return carry

    lax.fori_loop(0, LEVELS, edge_rows, 0)

    halos = [
        send(pe_out, pe_ref, 3, (lat, west)),
        send(pw_out, pw_ref, 4, (lat, east)),
        send(rows_out.at[0], north_ref, 5, (south, lon)),
        send(rows_out.at[1], south_ref, 6, (north, lon)),
        send(nc_out, ncs_ref, 7, (north, lon)),
    ]

    for n in (2, 1, 3):
        links[n].wait()
        remap(n, RL.at[n - 1])

    left = lax.broadcasted_iota(jnp.int32, (16, cols), 1) < 64
    for a in range(2):
        for f in range(FIELDS):
            for i in range(4):
                surf_ref[f, pl.ds((1 - a) * 64 + i, 16, stride=4), :] = jnp.where(left, Q[2 * a + 1, f, i], Q[2 * a, f, i])

    for c in halos:
        c.wait()
    below = jnp.where(lat > 0, 1.0, 0.0)
    over = jnp.where(lat < nlat - 1, 1.0, 0.0)
    south_ref[...] = south_ref[...] * below
    ncs_ref[...] = ncs_ref[...] * below
    north_ref[...] = north_ref[...] * over


def exchange(tracers, ec, nc, fluxes, source_cell, link_weight, target_cell):
    any_ = pl.BlockSpec(memory_space=pl.ANY)
    vm = pl.BlockSpec(memory_space=pltpu.VMEM)
    f = jnp.float32
    s = jax.ShapeDtypeStruct
    return pl.pallas_call(
        exchange_kernel,
        out_shape=[s((FIELDS, 128, 128), f), s((2, 128, 128), f), s((2, 128, 128), f), s((2, LEVELS, 2, 128), f),
                   s((2, LEVELS, 2, 128), f), s((LEVELS, 1, 128), f)],
        in_specs=[any_] * 3 + [vm] * 4,
        out_specs=[vm] * 6,
        scratch_shapes=[
            pltpu.VMEM((2, LEVELS, 128, 128), f),
            pltpu.VMEM((LEVELS, 128, 128), f),
            pltpu.VMEM((LEVELS, 8, 128), f),
            pltpu.VMEM((4, LINK_ROWS, 128), f),
            pltpu.VMEM((3, LINK_ROWS, 128), f),
            pltpu.VMEM((4, CAP_ROWS, 128), jnp.int32),
            pltpu.VMEM((2 * FIELDS, CAP_ROWS, 128), f),
            pltpu.VMEM((2 * FIELDS * 16, 6144), jnp.bfloat16),
            pltpu.VMEM((256, 6144), jnp.bfloat16),
            pltpu.VMEM((4, FIELDS, 4, 16, 128), f),
            pltpu.VMEM((2, 128, 128), f),
            pltpu.VMEM((2, 128, 128), f),
            pltpu.VMEM((2, 2, LEVELS, 2, 128), f),
            pltpu.VMEM((LEVELS, 1, 128), f),
            pltpu.SemaphoreType.DMA((3,)),
            pltpu.SemaphoreType.DMA((8,)),
            pltpu.SemaphoreType.DMA((8,)),
        ],
        compiler_params=pltpu.CompilerParams(collective_id=0, has_side_effects=True, vmem_limit_bytes=40 << 20),
        name="exchange",
    )(tracers, ec, nc, fluxes, source_cell, link_weight, target_cell)


def local(tracers, east_courant, north_courant, diffusivity, land_sea, fluxes, source_cell, link_weight, target_cell):
    surf, pe, pw, south, north, ncs = exchange(
        tracers, east_courant, north_courant, fluxes, source_cell, link_weight, target_cell)
    return column_step(tracers, east_courant, north_courant, diffusivity, land_sea, surf, pe, pw, south, north, ncs)


def solution(mesh):
    in_specs = (
        P(None, None, "lat", "lon"),
        P(None, "lat", "lon"),
        P(None, "lat", "lon"),
        P(None, "lat", "lon"),
        P("lat", "lon"),
        P(None, ("lat", "lon")),
        P(("lat", "lon"), None, None),
        P(("lat", "lon"), None, None),
        P(("lat", "lon"), None, None),
    )
    out_specs = P(None, None, "lat", "lon")
    return jax.shard_map(local, mesh=mesh, in_specs=in_specs, out_specs=out_specs, check_vma=False)
```

profile of v0, /device:TPU:0, one launch (start us, length us, event | category | flops | bytes accessed | tf_op | source)
XLA Modules:
  0.0 58.4 jit_solution(9252214662815900687)
XLA Ops:
  0.0 0.0 copy-start
  0.0 2.8 %copy-done = f32[2,48,128,128]{3,2,1,0:T(8,128)S(1)} copy-done((f32[2,48,128,128]{3,2,1,0:T(8,128)S(1)}, f32[2,48,128,128]{3,2,1,0:T(8,128)}, u32[]{:S(2)}) %copy-start) | copy-done | bytes 6291480
  2.8 0.0 copy-start.1
  2.8 1.9 %copy-done.1 = f32[48,128,128]{2,1,0:T(8,128)S(1)} copy-done((f32[48,128,128]{2,1,0:T(8,128)S(1)}, f32[48,128,128]{2,1,0:T(8,128)}, u32[]{:S(2)}) %copy-start.1) | copy-done | bytes 3145752
  4.7 0.0 copy-start.2
  4.7 1.9 %copy-done.2 = f32[48,128,128]{2,1,0:T(8,128)S(1)} copy-done((f32[48,128,128]{2,1,0:T(8,128)S(1)}, f32[48,128,128]{2,1,0:T(8,128)}, u32[]{:S(2)}) %copy-start.2) | copy-done | bytes 3145752
  6.6 0.0 copy-start.4
  6.6 0.9 %copy-done.4 = f32[6,8192]{1,0:T(8,128)S(1)} copy-done((f32[6,8192]{1,0:T(8,128)S(1)}, f32[6,8192]{1,0:T(8,128)}, u32[]{:S(2)}) %copy-start.4) | copy-done | bytes 196632
  7.5 0.0 copy-start.5
  7.5 0.9 %copy-done.5 = s32[1,4,6144]{2,1,0:T(4,128)S(1)} copy-done((s32[1,4,6144]{2,1,0:T(4,128)S(1)}, s32[1,4,6144]{2,1,0:T(4,128)}, u32[]{:S(2)}) %copy-start.5) | copy-done | bytes 98328
  8.4 0.0 copy-start.6
  8.4 0.9 %copy-done.6 = f32[1,4,6144]{2,1,0:T(4,128)S(1)} copy-done((f32[1,4,6144]{2,1,0:T(4,128)S(1)}, f32[1,4,6144]{2,1,0:T(4,128)}, u32[]{:S(2)}) %copy-start.6) | copy-done | bytes 98328
  9.3 0.0 copy-start.7
  9.3 0.9 %copy-done.7 = s32[1,4,6144]{2,1,0:T(4,128)S(1)} copy-done((s32[1,4,6144]{2,1,0:T(4,128)S(1)}, s32[1,4,6144]{2,1,0:T(4,128)}, u32[]{:S(2)}) %copy-start.7) | copy-done | bytes 98328
  10.2 0.0 copy-start.3
  10.2 0.0 copy-start.8
  10.2 32.7 %exchange.1 = (f32[5,128,128]{2,1,0:T(8,128)S(1)}, f32[2,128,128]{2,1,0:T(8,128)S(1)}, f32[2,128,128]{2,1,0:T(8,128)S(1)}, f32[2,48,2,128]{3,2,1,0:T(2,128)S(1)}...) custom-call(f32[2,48,128,128]{3,2,1,0:T(8,128)S(1)} %copy-done, f32[48,128,128]{2,1,0:T(8,128)S(1)} %copy-done.1, ...), custom_call_target="tpu_custom_call" | custom-call | tf_op jit(solution)/shard_map/exchange/pallas_call | solution.py:396
  42.9 0.0 copy-done.3
  42.9 0.0 copy-done.8
  42.9 15.5 %column_step.1 = f32[2,48,128,128]{3,2,1,0:T(8,128)} custom-call(f32[2,48,128,128]{3,2,1,0:T(8,128)} %tr_hbm.3, f32[48,128,128]{2,1,0:T(8,128)} %ec_hbm.3, f32[48,128,128]{2,1,0:T(8,128)} %nc_hbm.3, f32[48,128,128]{2,1,0:T(8,128)} %df_hbm.1, bf16[2,512,256]{2,1,0:T(8,128)(2,1)S(1)} %copy-done.3, s32[128,128]{1,0:T(8,128)S(1)} %copy-done.8, ...), custom_call_target="tpu_custom_call" | custom-call | tf_op jit(solution)/shard_map/column_step/pallas_call | solution.py:189
Async XLA Ops:
  0.0 2.8 %copy-start = (f32[2,48,128,128]{3,2,1,0:T(8,128)S(1)}, f32[2,48,128,128]{3,2,1,0:T(8,128)}, u32[]{:S(2)}) copy-start(f32[2,48,128,128]{3,2,1,0:T(8,128)} %tr_hbm.3) | copy-start | bytes 18874372
  2.8 1.9 %copy-start.1 = (f32[48,128,128]{2,1,0:T(8,128)S(1)}, f32[48,128,128]{2,1,0:T(8,128)}, u32[]{:S(2)}) copy-start(f32[48,128,128]{2,1,0:T(8,128)} %ec_hbm.3) | copy-start | bytes 9437188
  4.7 1.9 %copy-start.2 = (f32[48,128,128]{2,1,0:T(8,128)S(1)}, f32[48,128,128]{2,1,0:T(8,128)}, u32[]{:S(2)}) copy-start(f32[48,128,128]{2,1,0:T(8,128)} %nc_hbm.3) | copy-start | bytes 9437188
  6.6 0.9 %copy-start.4 = (f32[6,8192]{1,0:T(8,128)S(1)}, f32[6,8192]{1,0:T(8,128)}, u32[]{:S(2)}) copy-start(f32[6,8192]{1,0:T(8,128)} %flux_ref.1) | copy-start | bytes 589828
  7.5 0.9 %copy-start.5 = (s32[1,4,6144]{2,1,0:T(4,128)S(1)}, s32[1,4,6144]{2,1,0:T(4,128)}, u32[]{:S(2)}) copy-start(s32[1,4,6144]{2,1,0:T(4,128)} %src_ref.1) | copy-start | bytes 294916
  8.4 0.9 %copy-start.6 = (f32[1,4,6144]{2,1,0:T(4,128)S(1)}, f32[1,4,6144]{2,1,0:T(4,128)}, u32[]{:S(2)}) copy-start(f32[1,4,6144]{2,1,0:T(4,128)} %wgt_ref.1) | copy-start | bytes 294916
  9.3 0.9 %copy-start.7 = (s32[1,4,6144]{2,1,0:T(4,128)S(1)}, s32[1,4,6144]{2,1,0:T(4,128)}, u32[]{:S(2)}) copy-start(s32[1,4,6144]{2,1,0:T(4,128)} %tgt_ref.1) | copy-start | bytes 294916
  10.2 32.7 %copy-start.3 = (bf16[2,512,256]{2,1,0:T(8,128)(2,1)S(1)}, bf16[2,512,256]{2,1,0:T(8,128)(2,1)}, u32[]{:S(2)}) copy-start(bf16[2,512,256]{2,1,0:T(8,128)(2,1)} %constant.2.clone.w_ref) | copy-start | bytes 1572868
  10.2 32.7 %copy-start.8 = (s32[128,128]{1,0:T(8,128)S(1)}, s32[128,128]{1,0:T(8,128)}, u32[]{:S(2)}) copy-start(s32[128,128]{1,0:T(8,128)} %land_ref.1) | copy-start | bytes 196612
where the time goes:
time: 58.8 us; the launch traced here: 58.4 us
  Pallas kernels  48.2 us (82%)
  local copies, waits for them, and re-layouts  10.2 us (17%)
    pallas_call x1, Pallas kernels, exchange(): pl.pallas_call(exchange_kernel, out_shape=[s((FIELDS, 128, 128), f), s((2...  32.7 us
    pallas_call x1, Pallas kernels, column_step(): pl.pallas_call(column_kernel, out_shape=jax.ShapeDtypeStruct(tracers.shap...  15.5 us
    unnamed x18, local copies, waits for them, and re-layouts  10.2 us

commit v1 on v0

--- a/solution.py
+++ b/solution.py
@@ -42,25 +42,36 @@
 
 
 def column_kernel(tr_hbm, ec_hbm, nc_hbm, df_hbm, w_ref, land_ref, surf_ref, pe_ref, pw_ref, south_ref, north_ref, ncs_ref,
-                  out_hbm, T, EC, NC, DF, C, OUT, H, X, S, FN, in_sem, out_sem):
+                  out_hbm, T, EC, NC, DF, C, OUT, H, X, S, FN, tr_sem, co_sem, df_sem, out_sem):
     rows, cols = 128, 128
     blocks = rows // R
 
-    def loads(b):
-        r = pl.multiple_of(b * R, R)
-        return [
-            pltpu.make_async_copy(tr_hbm.at[:, :, pl.ds(r, R), :], T.at[:, :, pl.ds(r + PAD, R), :], in_sem.at[b, 0]),
-            pltpu.make_async_copy(ec_hbm.at[:, pl.ds(r, R), :], EC.at[:, pl.ds(r, R), :], in_sem.at[b, 1]),
-            pltpu.make_async_copy(nc_hbm.at[:, pl.ds(r, R), :], NC.at[:, pl.ds(r, R), :], in_sem.at[b, 2]),
-            pltpu.make_async_copy(df_hbm.at[:, pl.ds(r, R), :], DF.at[:, pl.ds(r, R), :], in_sem.at[b, 3]),
-        ]
-
-    def start(b, carry):
-        for c in loads(b):
+    groups = LEVELS // G
+
+    def span(i, size):
+        return pl.ds(pl.multiple_of(i * size, size), size)
+
+    def load_tracers(b, g):
+        return pltpu.make_async_copy(
+            tr_hbm.at[:, span(g, G), span(b, R), :],
+            T.at[:, span(g, G), pl.ds(pl.multiple_of(b * R + PAD, PAD), R), :], tr_sem.at[b, g])
+
+    def load_courants(b, g):
+        return [pltpu.make_async_copy(h.at[span(g, G), span(b, R), :], v.at[span(g, G), span(b, R), :], co_sem.at[p, b, g])
+                for p, (h, v) in enumerate(((ec_hbm, EC), (nc_hbm, NC)))]
+
+    def load_diffusivity(b):
+        return pltpu.make_async_copy(df_hbm.at[:, span(b, R), :], DF.at[:, span(b, R), :], df_sem.at[b])
+
+    def start_first(g, carry):
+        load_tracers(0, g).start()
+        load_tracers(1, g).start()
+        for c in load_courants(0, g):
             c.start()
         return carry
 
-    lax.fori_loop(0, blocks, start, 0)
+    lax.fori_loop(0, groups, start_first, 0)
+    load_diffusivity(0).start()
 
     lane = lax.broadcasted_iota(jnp.int32, (rows, cols), 1)
     low = lane % 4 < 2
@@ -70,25 +81,32 @@
             h = jnp.where(low, pw, pe) if half == 0 else jnp.where(low, pe, pw)
             H[t, half, 0], H[t, half, 1] = two_pieces(h)
 
-    for c in loads(0):
-        c.wait()
-
-    def edges(k, carry):
+    def pad_rows(k, carry):
         for t in range(2):
             T[t, k, PAD - 2:PAD, :] = south_ref[t, k]
             T[t, k, PAD + rows:PAD + rows + 2, :] = north_ref[t, k]
-            s = T[t, k, PAD - 2:PAD - 1, :] + T[t, k, PAD + 1:PAD + 2, :]
-            m = T[t, k, PAD - 1:PAD, :] + T[t, k, PAD:PAD + 1, :]
-            FN[t, k, PAD - 1:PAD, :] = ncs_ref[k] * (7.0 * m - s)
         return carry
 
-    lax.fori_loop(0, LEVELS, edges, 0)
+    lax.fori_loop(0, LEVELS, pad_rows, 0)
 
     def block(b, carry):
+        @pl.when((b > 0) & (b + 1 < blocks))
+        def _():
+            def start_next(g, carry):
+                load_tracers(b + 1, g).start()
+                return carry
+
+            lax.fori_loop(0, groups, start_next, 0)
+
         @pl.when(b + 1 < blocks)
         def _():
-            for c in loads(b + 1):
-                c.wait()
+            def start_next(g, carry):
+                for c in load_courants(b + 1, g):
+                    c.start()
+                return carry
+
+            lax.fori_loop(0, groups, start_next, 0)
+            load_diffusivity(b + 1).start()
 
         r = pl.multiple_of(b * R, R)
         rr = pl.ds(r, R)
@@ -98,6 +116,28 @@
 
         for half in range(2):
             def group(q, carry):
+                g = half * (HALF // G) + q
+
+                @pl.when(b == 0)
+                def _():
+                    load_tracers(0, g).wait()
+
+                @pl.when(b + 1 < blocks)
+                def _():
+                    load_tracers(b + 1, g).wait()
+
+                for c in load_courants(b, g):
+                    c.wait()
+
+                @pl.when(b == 0)
+                def _():
+                    for u in range(G):
+                        k = g * G + u
+                        for t in range(2):
+                            s = T[t, k, PAD - 2:PAD - 1, :] + T[t, k, PAD + 1:PAD + 2, :]
+                            m = T[t, k, PAD - 1:PAD, :] + T[t, k, PAD:PAD + 1, :]
+                            FN[t, k, PAD - 1:PAD, :] = ncs_ref[k] * (7.0 * m - s)
+
                 for u in range(G):
                     j = q * G + u
                     k = half * HALF + j
@@ -132,6 +172,7 @@
 
             lax.fori_loop(0, HALF // G, group, 0)
 
+        load_diffusivity(b).wait()
         heat = 0.5 * surf_ref[2, rr, :]
         tops = [0.5 * surf_ref[0, rr, :], 0.5 * surf_ref[1, rr, :]]
         above = None
@@ -182,7 +223,7 @@
 
 
 def column_step(tracers, ec, nc, df, land, surf, pe, pw, south, north, ncs):
-    any_ = pl.BlockSpec(memory_space=pl.ANY)
+    any_ = pl.BlockSpec(memory_space=pltpu.HBM)
     vm = pl.BlockSpec(memory_space=pltpu.VMEM)
     blocks = 128 // R
     f = jnp.float32
@@ -202,10 +243,12 @@
             pltpu.VMEM((2 * G * R, 512), jnp.bfloat16),
             pltpu.VMEM((2 * G * R, 256), f),
             pltpu.VMEM((2, LEVELS, 136, 128), f),
-            pltpu.SemaphoreType.DMA((blocks, 4)),
+            pltpu.SemaphoreType.DMA((blocks, LEVELS // G)),
+            pltpu.SemaphoreType.DMA((2, blocks, LEVELS // G)),
+            pltpu.SemaphoreType.DMA((blocks,)),
             pltpu.SemaphoreType.DMA((blocks,)),
         ],
-        compiler_params=pltpu.CompilerParams(vmem_limit_bytes=52 << 20),
+        compiler_params=pltpu.CompilerParams(vmem_limit_bytes=60 << 20),
         name="column_step",
     )(tracers, ec, nc, df, stencil_weights(), land, surf, pe, pw, south, north, ncs)
 FIELDS = 5
@@ -216,9 +259,10 @@
 MESH = pl.DeviceIdType.MESH
 
 
-def exchange_kernel(tr_hbm, ec_hbm, nc_hbm, flux_ref, src_ref, wgt_ref, tgt_ref,
+def exchange_kernel(tr_hbm, ec_hbm, nc_hbm, flux_hbm, src_hbm, wgt_hbm, tgt_hbm,
                     surf_ref, pe_ref, pw_ref, south_ref, north_ref, ncs_ref,
-                    T, EC, NC, L, RL, TG, WP, Z, B, Q, pe_out, pw_out, rows_out, nc_out, load_sem, send_sem, recv_sem):
+                    T, EC, NC, flux_ref, src_ref, wgt_ref, tgt_ref,
+                    L, RL, TG, WP, Z, B, Q, pe_out, pw_out, rows_out, nc_out, load_sem, send_sem, recv_sem):
     rows, cols = 128, 128
     lat, lon = lax.axis_index("lat"), lax.axis_index("lon")
     nlat, nlon = lax.axis_size("lat"), lax.axis_size("lon")
@@ -226,9 +270,13 @@
     east, west = lax.rem(lon + 1, nlon), lax.rem(lon + nlon - 1, nlon)
 
     loads = [
-        pltpu.make_async_copy(tr_hbm, T, load_sem.at[0]),
-        pltpu.make_async_copy(ec_hbm, EC, load_sem.at[1]),
-        pltpu.make_async_copy(nc_hbm.at[:, rows - 8:rows, :], NC, load_sem.at[2]),
+        pltpu.make_async_copy(src_hbm, src_ref, load_sem.at[0]),
+        pltpu.make_async_copy(wgt_hbm, wgt_ref, load_sem.at[1]),
+        pltpu.make_async_copy(flux_hbm, flux_ref, load_sem.at[2]),
+        pltpu.make_async_copy(tgt_hbm, tgt_ref, load_sem.at[3]),
+        pltpu.make_async_copy(tr_hbm, T, load_sem.at[4]),
+        pltpu.make_async_copy(ec_hbm, EC, load_sem.at[5]),
+        pltpu.make_async_copy(nc_hbm.at[:, rows - 8:rows, :], NC, load_sem.at[6]),
     ]
     for c in loads:
         c.start()
@@ -237,6 +285,8 @@
     for peer in ((lat, east), (lat, west), (north, lon), (south, lon), (north, east), (south, west)):
         pl.semaphore_signal(barrier, inc=1, device_id=peer, device_id_type=MESH)
 
+    for c in loads[:4]:
+        c.wait()
     field = lax.broadcasted_iota(jnp.int32, (8, cols), 0)
     for n in range(4):
         for h in range(16):
@@ -265,7 +315,10 @@
         3: send(L.at[3], RL.at[2], 2, (north, east)),
     }
 
+    b16 = jnp.bfloat16
     sub16 = lax.broadcasted_iota(jnp.int32, (16, cols), 0).astype(jnp.float32)
+    subs = [(sub16 + 16.0 * s).astype(b16) for s in range(16)]
+    one, zero16 = jnp.ones((16, cols), b16), jnp.zeros((16, cols), b16)
 
     def remap(n, box):
         exists = jnp.where(lat >= n // 2, 1.0, 0.0)
@@ -296,13 +349,13 @@
                 cell = TG[n, pl.ds(j, 1), :]
                 row = (cell >> 7) & 63
                 col = cell & 63
-                a = jnp.broadcast_to((row >> 2).astype(jnp.float32), (16, cols)) == sub16
-                b = jnp.broadcast_to((((row & 3) << 6) + col).astype(jnp.float32), (16, cols))
+                a = jnp.broadcast_to((row >> 2).astype(jnp.float32), (16, cols)).astype(b16) == subs[0]
+                b = jnp.broadcast_to((((row & 3) << 6) + col).astype(jnp.float32), (16, cols)).astype(b16)
                 for w in range(2 * FIELDS):
-                    v = jnp.broadcast_to(WP[w, pl.ds(j, 1), :], (16, cols))
-                    Z[w * 16:(w + 1) * 16, lanes] = jnp.where(a, v, 0.0).astype(jnp.bfloat16)
+                    v = jnp.broadcast_to(WP[w, pl.ds(j, 1), :], (16, cols)).astype(b16)
+                    Z[w * 16:(w + 1) * 16, lanes] = jnp.where(a, v, zero16)
                 for s in range(16):
-                    B[s * 16:(s + 1) * 16, lanes] = jnp.where(b == sub16 + 16.0 * s, 1.0, 0.0).astype(jnp.bfloat16)
+                    B[s * 16:(s + 1) * 16, lanes] = jnp.where(b == subs[s], one, zero16)
             return carry
 
         lax.fori_loop(0, CAP_ROWS // 4, hot, 0)
@@ -318,7 +371,7 @@
 
     remap(0, L.at[0])
 
-    for c in loads:
+    for c in loads[4:]:
         c.wait()
     lane = lax.broadcasted_iota(jnp.int32, (64, cols), 1)
     for t in range(2):
@@ -389,7 +442,7 @@
 
 
 def exchange(tracers, ec, nc, fluxes, source_cell, link_weight, target_cell):
-    any_ = pl.BlockSpec(memory_space=pl.ANY)
+    hbm = pl.BlockSpec(memory_space=pltpu.HBM)
     vm = pl.BlockSpec(memory_space=pltpu.VMEM)
     f = jnp.float32
     s = jax.ShapeDtypeStruct
@@ -397,12 +450,16 @@
         exchange_kernel,
         out_shape=[s((FIELDS, 128, 128), f), s((2, 128, 128), f), s((2, 128, 128), f), s((2, LEVELS, 2, 128), f),
                    s((2, LEVELS, 2, 128), f), s((LEVELS, 1, 128), f)],
-        in_specs=[any_] * 3 + [vm] * 4,
+        in_specs=[hbm] * 7,
         out_specs=[vm] * 6,
         scratch_shapes=[
             pltpu.VMEM((2, LEVELS, 128, 128), f),
             pltpu.VMEM((LEVELS, 128, 128), f),
             pltpu.VMEM((LEVELS, 8, 128), f),
+            pltpu.VMEM((6, 8192), f),
+            pltpu.VMEM((1, 4, 6144), jnp.int32),
+            pltpu.VMEM((1, 4, 6144), f),
+            pltpu.VMEM((1, 4, 6144), jnp.int32),
             pltpu.VMEM((4, LINK_ROWS, 128), f),
             pltpu.VMEM((3, LINK_ROWS, 128), f),
             pltpu.VMEM((4, CAP_ROWS, 128), jnp.int32),
@@ -414,11 +471,11 @@
             pltpu.VMEM((2, 128, 128), f),
             pltpu.VMEM((2, 2, LEVELS, 2, 128), f),
             pltpu.VMEM((LEVELS, 1, 128), f),
-            pltpu.SemaphoreType.DMA((3,)),
+            pltpu.SemaphoreType.DMA((7,)),
             pltpu.SemaphoreType.DMA((8,)),
             pltpu.SemaphoreType.DMA((8,)),
         ],
-        compiler_params=pltpu.CompilerParams(collective_id=0, has_side_effects=True, vmem_limit_bytes=40 << 20),
+        compiler_params=pltpu.CompilerParams(collective_id=0, has_side_effects=True, vmem_limit_bytes=60 << 20),
         name="exchange",
     )(tracers, ec, nc, fluxes, source_cell, link_weight, target_cell)
 

time: 58.8 us -> 50.2 us (0.85)
  local copies, waits for them, and re-layouts: 10.2 us -> 0 us
  Pallas kernels: 48.2 us -> 50.1 us
    unnamed x18 -> x0, local copies, waits for them, and re-layouts: 10.2 us -> none
    pallas_call x1, Pallas kernels: 15.5 us -> 17.6 us  [column_step(): pl.pallas_call(column_kernel, out_shape=jax.ShapeDtypeStruct(tracers.shap...]
where the time goes in v1:
time: 50.2 us; the launch traced here: 50.1 us
  Pallas kernels  50.1 us (100%)
    pallas_call x1, Pallas kernels, exchange(): pl.pallas_call(exchange_kernel, out_shape=[s((FIELDS, 128, 128), f), s((2...  32.5 us
    pallas_call x1, Pallas kernels, column_step(): pl.pallas_call(column_kernel, out_shape=jax.ShapeDtypeStruct(tracers.shap...  17.6 us

profile of v1, /device:TPU:0, one launch (start us, length us, event | category | flops | bytes accessed | tf_op | source)
XLA Modules:
  0.0 50.1 jit_solution(10313907748978083722)
XLA Ops:
  0.0 32.5 %exchange.1 = (f32[5,128,128]{2,1,0:T(8,128)}, f32[2,128,128]{2,1,0:T(8,128)}, f32[2,128,128]{2,1,0:T(8,128)}, f32[2,48,2,128]{3,2,1,0:T(2,128)}, f32[2,48,2,128]{3,2,1,0:T(2,128)}, /*index=5*/f32[48,1,128]{2,1,0:T(1,128)}) custom-call(f32[2,48,128,128]{3,2,1,0:T(8,128)} %tr_hbm.3, f32[48,128,128]{2,1,0:T(8,128)} %ec_hbm.3, f32[48,128,128]{2,1,0:T(8,128)} %nc_hbm.3, ...), custom_call_target="tpu_custom_call" | custom-call | tf_op jit(solution)/shard_map/exchange/pallas_call | solution.py:449
  32.5 17.6 %column_step.1 = f32[2,48,128,128]{3,2,1,0:T(8,128)} custom-call(f32[2,48,128,128]{3,2,1,0:T(8,128)} %tr_hbm.3, f32[48,128,128]{2,1,0:T(8,128)} %ec_hbm.3, f32[48,128,128]{2,1,0:T(8,128)} %nc_hbm.3, f32[48,128,128]{2,1,0:T(8,128)} %df_hbm.1, bf16[2,512,256]{2,1,0:T(8,128)(2,1)} %constant.2.clone.w_ref, s32[128,128]{1,0:T(8,128)} %land_ref.1, ...), custom_call_target="tpu_custom_call" | custom-call | tf_op jit(solution)/shard_map/column_step/pallas_call | solution.py:230

commit v2 on v1

--- a/solution.py
+++ b/solution.py
@@ -9,7 +9,7 @@
 LEVELS = 48
 HALF = 24
 R = 32
-G = 8
+G = 12
 PAD = 8
 
 
@@ -63,15 +63,25 @@
     def load_diffusivity(b):
         return pltpu.make_async_copy(df_hbm.at[:, span(b, R), :], DF.at[:, span(b, R), :], df_sem.at[b])
 
-    def start_first(g, carry):
-        load_tracers(0, g).start()
-        load_tracers(1, g).start()
-        for c in load_courants(0, g):
-            c.start()
+    def start_block(b, carry):
+        def start_group(g, carry):
+            @pl.when(b == 0)
+            def _():
+                load_tracers(0, g).start()
+
+            @pl.when(b + 1 < blocks)
+            def _():
+                load_tracers(b + 1, g).start()
+
+            for c in load_courants(b, g):
+                c.start()
+            return carry
+
+        lax.fori_loop(0, groups, start_group, 0)
+        load_diffusivity(b).start()
         return carry
 
-    lax.fori_loop(0, groups, start_first, 0)
-    load_diffusivity(0).start()
+    lax.fori_loop(0, blocks, start_block, 0)
 
     lane = lax.broadcasted_iota(jnp.int32, (rows, cols), 1)
     low = lane % 4 < 2
@@ -90,24 +100,6 @@
     lax.fori_loop(0, LEVELS, pad_rows, 0)
 
     def block(b, carry):
-        @pl.when((b > 0) & (b + 1 < blocks))
-        def _():
-            def start_next(g, carry):
-                load_tracers(b + 1, g).start()
-                return carry
-
-            lax.fori_loop(0, groups, start_next, 0)
-
-        @pl.when(b + 1 < blocks)
-        def _():
-            def start_next(g, carry):
-                for c in load_courants(b + 1, g):
-                    c.start()
-                return carry
-
-            lax.fori_loop(0, groups, start_next, 0)
-            load_diffusivity(b + 1).start()
-
         r = pl.multiple_of(b * R, R)
         rr = pl.ds(r, R)
         lane = lax.broadcasted_iota(jnp.int32, (R, cols), 1)
@@ -141,7 +133,7 @@
                 for u in range(G):
                     j = q * G + u
                     k = half * HALF + j
-                    here = (lane + 2 * half) % cols // 4 == j
+                    here = ((lane + 2 * half) & (cols - 1)) >> 2 == j
                     for t in range(2):
                         x = T[t, k, pl.ds(r + PAD, R), :]
                         at = pl.ds((u * 2 + t) * R, R)
@@ -256,13 +248,14 @@
 SRC0 = 80
 WGT0 = 128
 LINK_ROWS = 176
+CHUNKS = 1
 MESH = pl.DeviceIdType.MESH
 
 
 def exchange_kernel(tr_hbm, ec_hbm, nc_hbm, flux_hbm, src_hbm, wgt_hbm, tgt_hbm,
                     surf_ref, pe_ref, pw_ref, south_ref, north_ref, ncs_ref,
                     T, EC, NC, flux_ref, src_ref, wgt_ref, tgt_ref,
-                    L, RL, TG, WP, Z, B, Q, pe_out, pw_out, rows_out, nc_out, load_sem, send_sem, recv_sem):
+                    L, RL, TG, WPa, WPb, TAa, TAb, TBa, TBb, Za, Zb, Ba, Bb, ACC, Q, pe_out, pw_out, rows_out, nc_out, load_sem, send_sem, recv_sem):
     rows, cols = 128, 128
     lat, lon = lax.axis_index("lat"), lax.axis_index("lon")
     nlat, nlon = lax.axis_size("lat"), lax.axis_size("lon")
@@ -320,56 +313,79 @@
     subs = [(sub16 + 16.0 * s).astype(b16) for s in range(16)]
     one, zero16 = jnp.ones((16, cols), b16), jnp.zeros((16, cols), b16)
 
-    def remap(n, box):
+    def pick(n, box, WP, TA, TB, g):
         exists = jnp.where(lat >= n // 2, 1.0, 0.0)
-
-        def pick(g, carry):
-            at = pl.ds(pl.multiple_of(g * 8, 8), 8)
-            cell = box[pl.ds(pl.multiple_of(SRC0 + g * 8, 8), 8), :].astype(jnp.int32)
-            weight = box[pl.ds(pl.multiple_of(WGT0 + g * 8, 8), 8), :] * exists
-            low = cell & 127
-            high = cell >> 7
-            for f in range(FIELDS):
-                got = jnp.zeros((8, cols), jnp.float32)
-                for h in range(16):
-                    row = jnp.broadcast_to(box[h * FIELDS + f:h * FIELDS + f + 1, :], (8, cols))
-                    got = jnp.where(high == h, jnp.take_along_axis(row, low, axis=1), got)
-                got = got * weight
-                top = got.astype(jnp.bfloat16).astype(jnp.float32)
-                WP[f, at, :] = top
-                WP[FIELDS + f, at, :] = got - top
-            return carry
-
-        lax.fori_loop(0, CAP_ROWS // 8, pick, 0)
-
-        def hot(q, carry):
-            for u in range(4):
-                j = q * 4 + u
-                lanes = pl.ds(pl.multiple_of(j * 128, 128), 128)
-                cell = TG[n, pl.ds(j, 1), :]
-                row = (cell >> 7) & 63
-                col = cell & 63
-                a = jnp.broadcast_to((row >> 2).astype(jnp.float32), (16, cols)).astype(b16) == subs[0]
-                b = jnp.broadcast_to((((row & 3) << 6) + col).astype(jnp.float32), (16, cols)).astype(b16)
-                for w in range(2 * FIELDS):
-                    v = jnp.broadcast_to(WP[w, pl.ds(j, 1), :], (16, cols)).astype(b16)
-                    Z[w * 16:(w + 1) * 16, lanes] = jnp.where(a, v, zero16)
-                for s in range(16):
-                    B[s * 16:(s + 1) * 16, lanes] = jnp.where(b == subs[s], one, zero16)
-            return carry
-
-        lax.fori_loop(0, CAP_ROWS // 4, hot, 0)
-        quad = lax.dot_general(Z[...], B[...], (((1,), (1,)), ((), ())), preferred_element_type=jnp.float32)
+        at = pl.ds(pl.multiple_of(g * 8, 8), 8)
+        target = TG[n, at, :]
+        row = (target >> 7) & 63
+        TA[at, :] = (row >> 2).astype(jnp.float32)
+        TB[at, :] = (((row & 3) << 6) + (target & 63)).astype(jnp.float32)
+        cell = box[pl.ds(pl.multiple_of(SRC0 + g * 8, 8), 8), :].astype(jnp.int32)
+        weight = box[pl.ds(pl.multiple_of(WGT0 + g * 8, 8), 8), :] * exists
+        low = cell & 127
+        high = cell >> 7
+        for f in range(FIELDS):
+            got = jnp.zeros((8, cols), jnp.float32)
+            for h in range(16):
+                line = jnp.broadcast_to(box[h * FIELDS + f:h * FIELDS + f + 1, :], (8, cols))
+                got = jnp.where(high == h, jnp.take_along_axis(line, low, axis=1), got)
+            got = got * weight
+            top = got.astype(b16).astype(jnp.float32)
+            WP[f, at, :] = top
+            WP[FIELDS + f, at, :] = got - top
+
+    def hot(WP, TA, TB, Z, B, g):
+        for u in range(8):
+            j = g * 8 + u
+            lanes = pl.ds(pl.multiple_of(j * 128, 128), 128)
+            a = jnp.broadcast_to(TA[pl.ds(j, 1), :], (16, cols)).astype(b16) == subs[0]
+            b = jnp.broadcast_to(TB[pl.ds(j, 1), :], (16, cols)).astype(b16)
+            for w in range(2 * FIELDS):
+                v = jnp.broadcast_to(WP[w, pl.ds(j, 1), :], (16, cols)).astype(b16)
+                Z[w * 16:(w + 1) * 16, lanes] = jnp.where(a, v, zero16)
+            for s in range(16):
+                B[s * 16:(s + 1) * 16, lanes] = jnp.where(b == subs[s], one, zero16)
+
+    def place(Z, B, g):
+        size = CAP_ROWS * 128 // CHUNKS
+        lanes = pl.ds(pl.multiple_of(g * size, size), size)
+        return lax.dot_general(Z[:, lanes], B[:, lanes], (((1,), (1,)), ((), ())), preferred_element_type=jnp.float32)
+
+    def spread(n):
         col0 = (1 - n % 2) * 64
         for f in range(FIELDS):
-            total = quad[f * 16:(f + 1) * 16] + quad[(FIELDS + f) * 16:(FIELDS + f + 1) * 16]
+            total = ACC[f * 16:(f + 1) * 16, :] + ACC[(FIELDS + f) * 16:(FIELDS + f + 1) * 16, :]
             for i in range(4):
                 part = total[:, (i // 2) * 128:(i // 2 + 1) * 128]
                 if (i % 2) * 64 != col0:
                     part = pltpu.roll(part, 64, 1)
                 Q[n, f, i] = part
 
-    remap(0, L.at[0])
+    order = (0, 2, 1, 3)
+    boxes = {0: L.at[0], 1: RL.at[0], 2: RL.at[1], 3: RL.at[2]}
+    words = ((WPa, TAa, TBa), (WPb, TAb, TBb))
+    hots = ((Za, Ba), (Zb, Bb))
+
+    def stage(i):
+        def body(g, carry):
+            if 0 <= i - 2 < 4:
+                part = place(*hots[i % 2], g)
+            for v in range(6 // CHUNKS):
+                if 0 <= i - 1 < 4:
+                    hot(*words[(i - 1) % 2], *hots[(i - 1) % 2], g * (6 // CHUNKS) + v)
+                if i < 4:
+                    pick(order[i], boxes[order[i]], *words[i % 2], g * (6 // CHUNKS) + v)
+            if 0 <= i - 2 < 4:
+                ACC[...] += part
+            return carry
+
+        if 0 <= i - 2 < 4:
+            ACC[...] = jnp.zeros(ACC.shape, jnp.float32)
+        lax.fori_loop(0, CHUNKS, body, 0)
+        if 0 <= i - 2 < 4:
+            spread(order[i - 2])
+
+    stage(0)
 
     for c in loads[4:]:
         c.wait()
@@ -422,9 +438,10 @@
         send(nc_out, ncs_ref, 7, (north, lon)),
     ]
 
-    for n in (2, 1, 3):
-        links[n].wait()
-        remap(n, RL.at[n - 1])
+    for i in range(1, 6):
+        if i < 4:
+            links[order[i]].wait()
+        stage(i)
 
     left = lax.broadcasted_iota(jnp.int32, (16, cols), 1) < 64
     for a in range(2):
@@ -464,8 +481,16 @@
             pltpu.VMEM((3, LINK_ROWS, 128), f),
             pltpu.VMEM((4, CAP_ROWS, 128), jnp.int32),
             pltpu.VMEM((2 * FIELDS, CAP_ROWS, 128), f),
+            pltpu.VMEM((2 * FIELDS, CAP_ROWS, 128), f),
+            pltpu.VMEM((CAP_ROWS, 128), f),
+            pltpu.VMEM((CAP_ROWS, 128), f),
+            pltpu.VMEM((CAP_ROWS, 128), f),
+            pltpu.VMEM((CAP_ROWS, 128), f),
+            pltpu.VMEM((2 * FIELDS * 16, 6144), jnp.bfloat16),
             pltpu.VMEM((2 * FIELDS * 16, 6144), jnp.bfloat16),
             pltpu.VMEM((256, 6144), jnp.bfloat16),
+            pltpu.VMEM((256, 6144), jnp.bfloat16),
+            pltpu.VMEM((2 * FIELDS * 16, 256), f),
             pltpu.VMEM((4, FIELDS, 4, 16, 128), f),
             pltpu.VMEM((2, 128, 128), f),
             pltpu.VMEM((2, 128, 128), f),

time: 50.2 us -> 38.8 us (0.77)
  Pallas kernels: 50.1 us -> 38.6 us
    pallas_call x1, Pallas kernels: 32.5 us -> 24.7 us  [exchange(): pl.pallas_call(exchange_kernel, out_shape=[s((FIELDS, 128, 128), f), s((2...]
    pallas_call x1, Pallas kernels: 17.6 us -> 13.9 us  [column_step(): pl.pallas_call(column_kernel, out_shape=jax.ShapeDtypeStruct(tracers.shap...]
where the time goes in v2:
time: 38.8 us; the launch traced here: 38.6 us
  Pallas kernels  38.6 us (99%)
    pallas_call x1, Pallas kernels, exchange(): pl.pallas_call(exchange_kernel, out_shape=[s((FIELDS, 128, 128), f), s((2...  24.7 us
    pallas_call x1, Pallas kernels, column_step(): pl.pallas_call(column_kernel, out_shape=jax.ShapeDtypeStruct(tracers.shap...  13.9 us

profile of v2, /device:TPU:0, one launch (start us, length us, event | category | flops | bytes accessed | tf_op | source)
XLA Modules:
  0.0 38.6 jit_solution(11915938252996629680)
XLA Ops:
  0.0 24.7 %exchange.1 = (f32[5,128,128]{2,1,0:T(8,128)}, f32[2,128,128]{2,1,0:T(8,128)}, f32[2,128,128]{2,1,0:T(8,128)}, f32[2,48,2,128]{3,2,1,0:T(2,128)}, f32[2,48,2,128]{3,2,1,0:T(2,128)}, /*index=5*/f32[48,1,128]{2,1,0:T(1,128)}) custom-call(f32[2,48,128,128]{3,2,1,0:T(8,128)} %tr_hbm.3, f32[48,128,128]{2,1,0:T(8,128)} %ec_hbm.3, f32[48,128,128]{2,1,0:T(8,128)} %nc_hbm.3, ...), custom_call_target="tpu_custom_call" | custom-call | tf_op jit(solution)/shard_map/exchange/pallas_call | solution.py:466
  24.7 13.9 %column_step.1 = f32[2,48,128,128]{3,2,1,0:T(8,128)} custom-call(f32[2,48,128,128]{3,2,1,0:T(8,128)} %tr_hbm.3, f32[48,128,128]{2,1,0:T(8,128)} %ec_hbm.3, f32[48,128,128]{2,1,0:T(8,128)} %nc_hbm.3, f32[48,128,128]{2,1,0:T(8,128)} %df_hbm.1, bf16[2,512,256]{2,1,0:T(8,128)(2,1)} %constant.2.clone.w_ref, s32[128,128]{1,0:T(8,128)} %land_ref.1, ...), custom_call_target="tpu_custom_call" | custom-call | tf_op jit(solution)/shard_map/column_step/pallas_call | solution.py:222

commit v3 on v2

--- a/solution.py
+++ b/solution.py
@@ -248,7 +248,6 @@
 SRC0 = 80
 WGT0 = 128
 LINK_ROWS = 176
-CHUNKS = 1
 MESH = pl.DeviceIdType.MESH
 
 
@@ -292,21 +291,6 @@
             L[n, SRC0 + j:SRC0 + j + 1, :] = (src_ref[0, n:n + 1, lanes] - n * 2048).astype(jnp.float32)
             L[n, WGT0 + j:WGT0 + j + 1, :] = wgt_ref[0, n:n + 1, lanes]
             TG[n, j:j + 1, :] = tgt_ref[0, n:n + 1, lanes]
-
-    pl.semaphore_wait(barrier, 6)
-
-    def send(src, dst, at, peer):
-        copy = pltpu.make_async_remote_copy(
-            src_ref=src, dst_ref=dst, send_sem=send_sem.at[at], recv_sem=recv_sem.at[at],
-            device_id=peer, device_id_type=MESH)
-        copy.start()
-        return copy
-
-    links = {
-        1: send(L.at[1], RL.at[0], 0, (lat, east)),
-        2: send(L.at[2], RL.at[1], 1, (north, lon)),
-        3: send(L.at[3], RL.at[2], 2, (north, east)),
-    }
 
     b16 = jnp.bfloat16
     sub16 = lax.broadcasted_iota(jnp.int32, (16, cols), 0).astype(jnp.float32)
@@ -347,7 +331,7 @@
                 B[s * 16:(s + 1) * 16, lanes] = jnp.where(b == subs[s], one, zero16)
 
     def place(Z, B, g):
-        size = CAP_ROWS * 128 // CHUNKS
+        size = CAP_ROWS * 128
         lanes = pl.ds(pl.multiple_of(g * size, size), size)
         return lax.dot_general(Z[:, lanes], B[:, lanes], (((1,), (1,)), ((), ())), preferred_element_type=jnp.float32)
 
@@ -366,26 +350,39 @@
     words = ((WPa, TAa, TBa), (WPb, TAb, TBb))
     hots = ((Za, Ba), (Zb, Bb))
 
-    def stage(i):
+    def stage(picked, hotted, placed):
         def body(g, carry):
-            if 0 <= i - 2 < 4:
-                part = place(*hots[i % 2], g)
-            for v in range(6 // CHUNKS):
-                if 0 <= i - 1 < 4:
-                    hot(*words[(i - 1) % 2], *hots[(i - 1) % 2], g * (6 // CHUNKS) + v)
-                if i < 4:
-                    pick(order[i], boxes[order[i]], *words[i % 2], g * (6 // CHUNKS) + v)
-            if 0 <= i - 2 < 4:
-                ACC[...] += part
+            if placed is not None:
+                ACC[...] = place(*hots[placed % 2], g)
+            for v in range(CAP_ROWS // 8):
+                if hotted is not None:
+                    hot(*words[hotted % 2], *hots[hotted % 2], v)
+                if picked is not None:
+                    pick(order[picked], boxes[order[picked]], *words[picked % 2], v)
             return carry
 
-        if 0 <= i - 2 < 4:
-            ACC[...] = jnp.zeros(ACC.shape, jnp.float32)
-        lax.fori_loop(0, CHUNKS, body, 0)
-        if 0 <= i - 2 < 4:
-            spread(order[i - 2])
-
-    stage(0)
+        lax.fori_loop(0, 1, body, 0)
+        if placed is not None:
+            spread(order[placed])
+
+    stage(0, None, None)
+    stage(None, 0, None)
+
+    pl.semaphore_wait(barrier, 6)
+
+    def send(src, dst, at, peer):
+        copy = pltpu.make_async_remote_copy(
+            src_ref=src, dst_ref=dst, send_sem=send_sem.at[at], recv_sem=recv_sem.at[at],
+            device_id=peer, device_id_type=MESH)
+        copy.start()
+        return copy
+
+    links = {
+        1: send(L.at[1], RL.at[0], 0, (lat, east)),
+        2: send(L.at[2], RL.at[1], 1, (north, lon)),
+        3: send(L.at[3], RL.at[2], 2, (north, east)),
+    }
+
 
     for c in loads[4:]:
         c.wait()
@@ -438,10 +435,14 @@
         send(nc_out, ncs_ref, 7, (north, lon)),
     ]
 
-    for i in range(1, 6):
-        if i < 4:
-            links[order[i]].wait()
-        stage(i)
+    links[order[1]].wait()
+    stage(1, None, 0)
+    links[order[2]].wait()
+    stage(2, 1, None)
+    links[order[3]].wait()
+    stage(3, 2, 1)
+    stage(None, 3, 2)
+    stage(None, None, 3)
 
     left = lax.broadcasted_iota(jnp.int32, (16, cols), 1) < 64
     for a in range(2):

time: 38.8 us -> 36.9 us (0.951)
  Pallas kernels: 38.6 us -> 36.8 us
    pallas_call x1, Pallas kernels: 24.7 us -> 22.8 us  [exchange(): pl.pallas_call(exchange_kernel, out_shape=[s((FIELDS, 128, 128), f), s((2...]
where the time goes in v3:
time: 36.9 us; the launch traced here: 36.8 us
  Pallas kernels  36.8 us (100%)
    pallas_call x1, Pallas kernels, exchange(): pl.pallas_call(exchange_kernel, out_shape=[s((FIELDS, 128, 128), f), s((2...  22.8 us
    pallas_call x1, Pallas kernels, column_step(): pl.pallas_call(column_kernel, out_shape=jax.ShapeDtypeStruct(tracers.shap...  13.9 us

profile of v3, /device:TPU:0, one launch (start us, length us, event | category | flops | bytes accessed | tf_op | source)
XLA Modules:
  0.0 36.8 jit_solution(10249931671543870189)
XLA Ops:
  0.0 22.8 %exchange.1 = (f32[5,128,128]{2,1,0:T(8,128)}, f32[2,128,128]{2,1,0:T(8,128)}, f32[2,128,128]{2,1,0:T(8,128)}, f32[2,48,2,128]{3,2,1,0:T(2,128)}, f32[2,48,2,128]{3,2,1,0:T(2,128)}, /*index=5*/f32[48,1,128]{2,1,0:T(1,128)}) custom-call(f32[2,48,128,128]{3,2,1,0:T(8,128)} %tr_hbm.3, f32[48,128,128]{2,1,0:T(8,128)} %ec_hbm.3, f32[48,128,128]{2,1,0:T(8,128)} %nc_hbm.3, ...), custom_call_target="tpu_custom_call" | custom-call | tf_op jit(solution)/shard_map/exchange/pallas_call | solution.py:467
  22.9 13.9 %column_step.1 = f32[2,48,128,128]{3,2,1,0:T(8,128)} custom-call(f32[2,48,128,128]{3,2,1,0:T(8,128)} %tr_hbm.3, f32[48,128,128]{2,1,0:T(8,128)} %ec_hbm.3, f32[48,128,128]{2,1,0:T(8,128)} %nc_hbm.3, f32[48,128,128]{2,1,0:T(8,128)} %df_hbm.1, bf16[2,512,256]{2,1,0:T(8,128)(2,1)} %constant.2.clone.w_ref, s32[128,128]{1,0:T(8,128)} %land_ref.1, ...), custom_call_target="tpu_custom_call" | custom-call | tf_op jit(solution)/shard_map/column_step/pallas_call | solution.py:222

commit v4 on v3

--- a/solution.py
+++ b/solution.py
@@ -41,8 +41,8 @@
     return high, (x - high.astype(jnp.float32)).astype(jnp.bfloat16)
 
 
-def column_kernel(tr_hbm, ec_hbm, nc_hbm, df_hbm, w_ref, land_ref, surf_ref, pe_ref, pw_ref, south_ref, north_ref, ncs_ref,
-                  out_hbm, T, EC, NC, DF, C, OUT, H, X, S, FN, tr_sem, co_sem, df_sem, out_sem):
+def column_kernel(tr_hbm, ec_hbm, nc_hbm, df_hbm, w_hbm, land_hbm, surf_hbm, pe_hbm, pw_hbm, south_hbm, north_hbm, ncs_hbm,
+                  out_hbm, w_ref, land_ref, surf_ref, pe_ref, pw_ref, south_ref, north_ref, ncs_ref, T, EC, NC, DF, C, OUT, H, X, S, FN, tr_sem, co_sem, df_sem, out_sem, small_sem):
     rows, cols = 128, 128
     blocks = rows // R
 
@@ -81,7 +81,19 @@
         load_diffusivity(b).start()
         return carry
 
-    lax.fori_loop(0, blocks, start_block, 0)
+    small = [
+        pltpu.make_async_copy(h, v, small_sem.at[p]) for p, (h, v) in enumerate((
+            (pe_hbm, pe_ref), (pw_hbm, pw_ref), (south_hbm, south_ref), (north_hbm, north_ref), (ncs_hbm, ncs_ref),
+            (w_hbm, w_ref), (surf_hbm, surf_ref), (land_hbm, land_ref)))
+    ]
+    for c in small[:6]:
+        c.start()
+    start_block(0, 0)
+    for c in small[6:]:
+        c.start()
+    lax.fori_loop(1, blocks, start_block, 0)
+    for c in small[:6]:
+        c.wait()
 
     lane = lax.broadcasted_iota(jnp.int32, (rows, cols), 1)
     low = lane % 4 < 2
@@ -104,7 +116,6 @@
         rr = pl.ds(r, R)
         lane = lax.broadcasted_iota(jnp.int32, (R, cols), 1)
         first = lane == 0
-        stress = 2.0 * jnp.sqrt(surf_ref[3, rr, :] * surf_ref[3, rr, :] + surf_ref[4, rr, :] * surf_ref[4, rr, :])
 
         for half in range(2):
             def group(q, carry):
@@ -165,6 +176,13 @@
             lax.fori_loop(0, HALF // G, group, 0)
 
         load_diffusivity(b).wait()
+
+        @pl.when(b == 0)
+        def _():
+            for c in small[6:]:
+                c.wait()
+
+        stress = 2.0 * jnp.sqrt(surf_ref[3, rr, :] * surf_ref[3, rr, :] + surf_ref[4, rr, :] * surf_ref[4, rr, :])
         heat = 0.5 * surf_ref[2, rr, :]
         tops = [0.5 * surf_ref[0, rr, :], 0.5 * surf_ref[1, rr, :]]
         above = None
@@ -216,15 +234,22 @@
 
 def column_step(tracers, ec, nc, df, land, surf, pe, pw, south, north, ncs):
     any_ = pl.BlockSpec(memory_space=pltpu.HBM)
-    vm = pl.BlockSpec(memory_space=pltpu.VMEM)
     blocks = 128 // R
     f = jnp.float32
     return pl.pallas_call(
         column_kernel,
         out_shape=jax.ShapeDtypeStruct(tracers.shape, f),
-        in_specs=[any_] * 4 + [vm] * 8,
+        in_specs=[any_] * 12,
         out_specs=any_,
         scratch_shapes=[
+            pltpu.VMEM((2, 512, 256), jnp.bfloat16),
+            pltpu.VMEM((128, 128), jnp.int32),
+            pltpu.VMEM((5, 128, 128), f),
+            pltpu.VMEM((2, 128, 128), f),
+            pltpu.VMEM((2, 128, 128), f),
+            pltpu.VMEM((2, LEVELS, 2, 128), f),
+            pltpu.VMEM((2, LEVELS, 2, 128), f),
+            pltpu.VMEM((LEVELS, 1, 128), f),
             pltpu.VMEM((2, LEVELS, 144, 128), f),
             pltpu.VMEM((LEVELS, 128, 128), f),
             pltpu.VMEM((LEVELS, 128, 128), f),
@@ -239,6 +264,7 @@
             pltpu.SemaphoreType.DMA((2, blocks, LEVELS // G)),
             pltpu.SemaphoreType.DMA((blocks,)),
             pltpu.SemaphoreType.DMA((blocks,)),
+            pltpu.SemaphoreType.DMA((8,)),
         ],
         compiler_params=pltpu.CompilerParams(vmem_limit_bytes=60 << 20),
         name="column_step",
@@ -252,9 +278,9 @@
 
 
 def exchange_kernel(tr_hbm, ec_hbm, nc_hbm, flux_hbm, src_hbm, wgt_hbm, tgt_hbm,
-                    surf_ref, pe_ref, pw_ref, south_ref, north_ref, ncs_ref,
-                    T, EC, NC, flux_ref, src_ref, wgt_ref, tgt_ref,
-                    L, RL, TG, WPa, WPb, TAa, TAb, TBa, TBb, Za, Zb, Ba, Bb, ACC, Q, pe_out, pw_out, rows_out, nc_out, load_sem, send_sem, recv_sem):
+                    surf_hbm, pe_hbm, pw_hbm, south_hbm, north_hbm, ncs_hbm,
+                    surf_ref, pe_ref, pw_ref, south_ref, north_ref, ncs_ref, T, EC, NC, flux_ref, src_ref, wgt_ref, tgt_ref,
+                    L, RL, TG, WPa, WPb, TAa, TAb, TBa, TBb, Za, Zb, Ba, Bb, ACC, Q, pe_out, pw_out, rows_out, nc_out, load_sem, send_sem, recv_sem, out_sem):
     rows, cols = 128, 128
     lat, lon = lax.axis_index("lat"), lax.axis_index("lon")
     nlat, nlon = lax.axis_size("lat"), lax.axis_size("lon")
@@ -442,14 +468,6 @@
     links[order[3]].wait()
     stage(3, 2, 1)
     stage(None, 3, 2)
-    stage(None, None, 3)
-
-    left = lax.broadcasted_iota(jnp.int32, (16, cols), 1) < 64
-    for a in range(2):
-        for f in range(FIELDS):
-            for i in range(4):
-                surf_ref[f, pl.ds((1 - a) * 64 + i, 16, stride=4), :] = jnp.where(left, Q[2 * a + 1, f, i], Q[2 * a, f, i])
-
     for c in halos:
         c.wait()
     below = jnp.where(lat > 0, 1.0, 0.0)
@@ -457,11 +475,28 @@
     south_ref[...] = south_ref[...] * below
     ncs_ref[...] = ncs_ref[...] * below
     north_ref[...] = north_ref[...] * over
+    results = [
+        pltpu.make_async_copy(v, h, out_sem.at[p]) for p, (v, h) in enumerate((
+            (pe_ref, pe_hbm), (pw_ref, pw_hbm), (south_ref, south_hbm), (north_ref, north_hbm), (ncs_ref, ncs_hbm),
+            (surf_ref, surf_hbm)))
+    ]
+    for c in results[:5]:
+        c.start()
+
+    stage(None, None, 3)
+
+    left = lax.broadcasted_iota(jnp.int32, (16, cols), 1) < 64
+    for a in range(2):
+        for f in range(FIELDS):
+            for i in range(4):
+                surf_ref[f, pl.ds((1 - a) * 64 + i, 16, stride=4), :] = jnp.where(left, Q[2 * a + 1, f, i], Q[2 * a, f, i])
+    results[5].start()
+    for c in results:
+        c.wait()
 
 
 def exchange(tracers, ec, nc, fluxes, source_cell, link_weight, target_cell):
     hbm = pl.BlockSpec(memory_space=pltpu.HBM)
-    vm = pl.BlockSpec(memory_space=pltpu.VMEM)
     f = jnp.float32
     s = jax.ShapeDtypeStruct
     return pl.pallas_call(
@@ -469,8 +504,14 @@
         out_shape=[s((FIELDS, 128, 128), f), s((2, 128, 128), f), s((2, 128, 128), f), s((2, LEVELS, 2, 128), f),
                    s((2, LEVELS, 2, 128), f), s((LEVELS, 1, 128), f)],
         in_specs=[hbm] * 7,
-        out_specs=[vm] * 6,
+        out_specs=[hbm] * 6,
         scratch_shapes=[
+            pltpu.VMEM((FIELDS, 128, 128), f),
+            pltpu.VMEM((2, 128, 128), f),
+            pltpu.VMEM((2, 128, 128), f),
+            pltpu.VMEM((2, LEVELS, 2, 128), f),
+            pltpu.VMEM((2, LEVELS, 2, 128), f),
+            pltpu.VMEM((LEVELS, 1, 128), f),
             pltpu.VMEM((2, LEVELS, 128, 128), f),
             pltpu.VMEM((LEVELS, 128, 128), f),
             pltpu.VMEM((LEVELS, 8, 128), f),
@@ -500,6 +541,7 @@
             pltpu.SemaphoreType.DMA((7,)),
             pltpu.SemaphoreType.DMA((8,)),
             pltpu.SemaphoreType.DMA((8,)),
+            pltpu.SemaphoreType.DMA((6,)),
         ],
         compiler_params=pltpu.CompilerParams(collective_id=0, has_side_effects=True, vmem_limit_bytes=60 << 20),
         name="exchange",

time: 36.9 us -> 36.5 us (0.989)
  Pallas kernels: 36.8 us -> 36.4 us
    pallas_call x1, Pallas kernels: 13.9 us -> 13.2 us  [column_step(): pl.pallas_call(column_kernel, out_shape=jax.ShapeDtypeStruct(tracers.shap...]
where the time goes in v4:
time: 36.5 us; the launch traced here: 36.4 us
  Pallas kernels  36.4 us (100%)
    pallas_call x1, Pallas kernels, exchange(): pl.pallas_call(exchange_kernel, out_shape=[s((FIELDS, 128, 128), f), s((2...  23.2 us
    pallas_call x1, Pallas kernels, column_step(): pl.pallas_call(column_kernel, out_shape=jax.ShapeDtypeStruct(tracers.shap...  13.2 us

profile of v4, /device:TPU:0, one launch (start us, length us, event | category | flops | bytes accessed | tf_op | source)
XLA Modules:
  0.0 36.4 jit_solution(14697727111318944314)
XLA Ops:
  0.0 23.2 %exchange.1 = (f32[5,128,128]{2,1,0:T(8,128)}, f32[2,128,128]{2,1,0:T(8,128)}, f32[2,128,128]{2,1,0:T(8,128)}, f32[2,48,2,128]{3,2,1,0:T(2,128)}, f32[2,48,2,128]{3,2,1,0:T(2,128)}, /*index=5*/f32[48,1,128]{2,1,0:T(1,128)}) custom-call(f32[2,48,128,128]{3,2,1,0:T(8,128)} %tr_hbm.3, f32[48,128,128]{2,1,0:T(8,128)} %ec_hbm.3, f32[48,128,128]{2,1,0:T(8,128)} %nc_hbm.3, ...), custom_call_target="tpu_custom_call" | custom-call | tf_op jit(solution)/shard_map/exchange/pallas_call | solution.py:502
  23.2 13.2 %column_step.1 = f32[2,48,128,128]{3,2,1,0:T(8,128)} custom-call(f32[2,48,128,128]{3,2,1,0:T(8,128)} %tr_hbm.3, f32[48,128,128]{2,1,0:T(8,128)} %ec_hbm.3, f32[48,128,128]{2,1,0:T(8,128)} %nc_hbm.3, f32[48,128,128]{2,1,0:T(8,128)} %df_hbm.1, bf16[2,512,256]{2,1,0:T(8,128)(2,1)} %constant.2.clone.w_hbm, s32[128,128]{1,0:T(8,128)} %land_hbm.1, ...), custom_call_target="tpu_custom_call" | custom-call | tf_op jit(solution)/shard_map/column_step/pallas_call | solution.py:239

commit v5 on v4

--- a/solution.py
+++ b/solution.py
@@ -103,13 +103,15 @@
             h = jnp.where(low, pw, pe) if half == 0 else jnp.where(low, pe, pw)
             H[t, half, 0], H[t, half, 1] = two_pieces(h)
 
-    def pad_rows(k, carry):
-        for t in range(2):
-            T[t, k, PAD - 2:PAD, :] = south_ref[t, k]
-            T[t, k, PAD + rows:PAD + rows + 2, :] = north_ref[t, k]
+    def pad_rows(q, carry):
+        for u in range(8):
+            k = q * 8 + u
+            for t in range(2):
+                T[t, k, PAD - 2:PAD, :] = south_ref[t, k]
+                T[t, k, PAD + rows:PAD + rows + 2, :] = north_ref[t, k]
         return carry
 
-    lax.fori_loop(0, LEVELS, pad_rows, 0)
+    lax.fori_loop(0, LEVELS // 8, pad_rows, 0)
 
     def block(b, carry):
         r = pl.multiple_of(b * R, R)
@@ -444,18 +446,23 @@
             pe_out[t, rr, :] = pe
             pw_out[t, rr, :] = pw
 
-    def edge_rows(k, carry):
-        for t in range(2):
-            rows_out[0, t, k] = T[t, k, 0:2, :]
-            rows_out[1, t, k] = T[t, k, rows - 2:rows, :]
-        nc_out[k] = NC[k, 7:8, :]
-        return carry
-
-    lax.fori_loop(0, LEVELS, edge_rows, 0)
-
-    halos = [
+    columns = [
         send(pe_out, pe_ref, 3, (lat, west)),
         send(pw_out, pw_ref, 4, (lat, east)),
+    ]
+
+    def edge_rows(q, carry):
+        for u in range(8):
+            k = q * 8 + u
+            for t in range(2):
+                rows_out[0, t, k] = T[t, k, 0:2, :]
+                rows_out[1, t, k] = T[t, k, rows - 2:rows, :]
+            nc_out[k] = NC[k, 7:8, :]
+        return carry
+
+    lax.fori_loop(0, LEVELS // 8, edge_rows, 0)
+
+    halos = [
         send(rows_out.at[0], north_ref, 5, (south, lon)),
         send(rows_out.at[1], south_ref, 6, (north, lon)),
         send(nc_out, ncs_ref, 7, (north, lon)),
@@ -468,7 +475,7 @@
     links[order[3]].wait()
     stage(3, 2, 1)
     stage(None, 3, 2)
-    for c in halos:
+    for c in columns + halos:
         c.wait()
     below = jnp.where(lat > 0, 1.0, 0.0)
     over = jnp.where(lat < nlat - 1, 1.0, 0.0)

time: 36.5 us -> 36.1 us (0.989)
  Pallas kernels: 36.4 us -> 36 us
where the time goes in v5:
time: 36.1 us; the launch traced here: 36 us
  Pallas kernels  36 us (100%)
    pallas_call x1, Pallas kernels, exchange(): pl.pallas_call(exchange_kernel, out_shape=[s((FIELDS, 128, 128), f), s((2...  22.9 us
    pallas_call x1, Pallas kernels, column_step(): pl.pallas_call(column_kernel, out_shape=jax.ShapeDtypeStruct(tracers.shap...  13.2 us

profile of v5, /device:TPU:0, one launch (start us, length us, event | category | flops | bytes accessed | tf_op | source)
XLA Modules:
  0.0 36.0 jit_solution(15562885412142450597)
XLA Ops:
  0.0 22.9 %exchange.1 = (f32[5,128,128]{2,1,0:T(8,128)}, f32[2,128,128]{2,1,0:T(8,128)}, f32[2,128,128]{2,1,0:T(8,128)}, f32[2,48,2,128]{3,2,1,0:T(2,128)}, f32[2,48,2,128]{3,2,1,0:T(2,128)}, /*index=5*/f32[48,1,128]{2,1,0:T(1,128)}) custom-call(f32[2,48,128,128]{3,2,1,0:T(8,128)} %tr_hbm.3, f32[48,128,128]{2,1,0:T(8,128)} %ec_hbm.3, f32[48,128,128]{2,1,0:T(8,128)} %nc_hbm.3, ...), custom_call_target="tpu_custom_call" | custom-call | tf_op jit(solution)/shard_map/exchange/pallas_call | solution.py:509
  22.9 13.2 %column_step.1 = f32[2,48,128,128]{3,2,1,0:T(8,128)} custom-call(f32[2,48,128,128]{3,2,1,0:T(8,128)} %tr_hbm.3, f32[48,128,128]{2,1,0:T(8,128)} %ec_hbm.3, f32[48,128,128]{2,1,0:T(8,128)} %nc_hbm.3, f32[48,128,128]{2,1,0:T(8,128)} %df_hbm.1, bf16[2,512,256]{2,1,0:T(8,128)(2,1)} %constant.2.clone.w_hbm, s32[128,128]{1,0:T(8,128)} %land_hbm.1, ...), custom_call_target="tpu_custom_call" | custom-call | tf_op jit(solution)/shard_map/column_step/pallas_call | solution.py:241
